TPU v7x, 512 devices: a whole 4x8x8 slice. The times are simulated.
512 devices in a mesh: row: 64 (over y_hi, x, z), col: 8 (over y_lo, core).
Axes of the slice: x: 4, y: 8 (y_hi: 2, y_lo: 4; y = y_hi * 4 + y_lo), z: 8, core: 2. Of those that a mesh axis runs over, the one named last changes fastest.
Arguments:
- features: bfloat16 [131072, 256], P(('row', 'col')), may hold values from -6 to 6
- weight: bfloat16 [256, 256], replicated, may hold values from -0.375 to 0.375
- weight_self: bfloat16 [256, 256], replicated, may hold values from -0.375 to 0.375
- tile_values: bfloat16 [64, 256, 128, 128], P('row', 'col'), may hold values from -0.125 to 0.125
- tile_rows: int32 [64, 256], P('row', 'col'), may hold values from 0 to 1
- tile_cols: int32 [64, 256], P('row', 'col'), may hold values from 0 to 47
- tile_count: int32 [64, 8], P('row', 'col'), may hold values from 1 to 32, as said below
- cotangent: bfloat16 [131072, 256], P(('row', 'col')), may hold values from -6 to 6
Outputs:
- activations: bfloat16 [131072, 256], P(('row', 'col'))
- feature_grad: bfloat16 [131072, 256], P(('row', 'col'))
- weight_grad: float32 [256, 256], replicated
- self_grad: float32 [256, 256], replicated
Inputs may be any that keep to these rules, and one draw needn't show every extreme that they name: Slots 0 to tile_count - 1 of a node block are live, the others are ignored; some node block has all 32 slots live.
All inputs are finite; a program needn't handle non-finite values.
Results may differ from a plain program's by a relative error of at most 0.0052.
Values may be sent and summed in bfloat16 or wider, within the bound.
A program may use at most 64 MiB of HBM per device.

v0:
```python
import math
import jax
import jax.numpy as jnp
from jax import lax
from jax.sharding import PartitionSpec as P


def with_halo(cells, sides, width):
    for axis, dim in sides:
        count = lax.axis_size(axis)
        head = lax.slice_in_dim(cells, 0, width, axis=dim)
        tail = lax.slice_in_dim(cells, cells.shape[dim] - width, cells.shape[dim], axis=dim)
        cells = jnp.concatenate(
            [
                lax.ppermute(tail, axis, [(i, (i + 1) % count) for i in range(count)]),
                cells,
                lax.ppermute(head, axis, [((i + 1) % count, i) for i in range(count)]),
            ],
            axis=dim,
        )
    return cells


def passed_along(value, axis, steps):
    count = lax.axis_size(axis)
    pairs = [(source, (source + steps) % count) for source in range(count)]
    return lax.ppermute(value, axis, pairs)


def shards(features, weight, weight_self, tile_values, tile_rows, tile_cols, tile_count, cotangent):
    tile_block = tile_values[0]
    slot_rows = tile_rows[0]
    slot_cols = tile_cols[0]
    live_count = tile_count[0, 0]
    slot_total = tile_block.shape[0]
    tile_side = tile_block.shape[-1]
    node_rows = features.shape[0]
    width = features.shape[1]
    per_block = node_rows // tile_side
    col_count = lax.axis_size("col")
    row_count = lax.axis_size("row")
    span = col_count * per_block
    group = lax.all_gather(features, "col", axis=0, tiled=True)
    window = with_halo(group, (("row", 0),), group.shape[0])
    window_tiles = window.reshape(-1, tile_side, width)
    row_ids = jnp.arange(per_block, dtype=jnp.int32)
    tiles_part = tile_block
    rows_part = slot_rows
    live_part = jnp.arange(slot_total, dtype=jnp.int32) < live_count
    feat_tiles = window_tiles[slot_cols]
    selector = ((rows_part[None, :] == row_ids[:, None]) & live_part[None, :]).astype(jnp.bfloat16)
    masked = tiles_part[None, :, :, :] * selector[:, :, None, None]
    summed = jnp.einsum("ktij,tjf->kif", masked, feat_tiles, preferred_element_type=jnp.float32)
    aggregated = summed.reshape(node_rows, width).astype(jnp.bfloat16)
    pre_act = jnp.dot(aggregated, weight, preferred_element_type=jnp.float32) + jnp.dot(
        features, weight_self, preferred_element_type=jnp.float32
    )
    activations = jax.nn.silu(pre_act).astype(jnp.bfloat16)
    sigma = jax.nn.sigmoid(pre_act)
    grad_pre = (cotangent.astype(jnp.float32) * sigma * (1.0 + pre_act * (1.0 - sigma))).astype(
        jnp.bfloat16
    )
    weight_part = jnp.einsum("nf,ng->fg", aggregated, grad_pre, preferred_element_type=jnp.float32)
    self_part = jnp.einsum("nf,ng->fg", features, grad_pre, preferred_element_type=jnp.float32)
    grad_aggregated = jnp.einsum(
        "ng,fg->nf", grad_pre, weight, preferred_element_type=jnp.float32
    ).astype(jnp.bfloat16)
    self_feature = jnp.einsum(
        "ng,fg->nf", grad_pre, weight_self, preferred_element_type=jnp.float32
    )
    grad_tiles = grad_aggregated.reshape(per_block, tile_side, width)
    spread_zero = jnp.zeros((3 * span, tile_side, width), jnp.float32)
    tiles_part = tile_block
    rows_part = slot_rows
    live_part = (jnp.arange(slot_total, dtype=jnp.int32) < live_count).astype(jnp.float32)
    picked = grad_tiles[rows_part]
    products = jnp.einsum("tij,tif->tjf", tiles_part, picked, preferred_element_type=jnp.float32)
    spread = spread_zero.at[slot_cols].add(products * live_part[:, None, None])
    spread = spread.reshape(3, col_count * node_rows, width)
    middle = spread[1]
    for offset in (1, -1):
        outgoing = spread[2] if offset == 1 else spread[0]
        middle = middle + passed_along(outgoing, "row", offset)
    own_share = lax.psum_scatter(middle, "col", scatter_dimension=0, tiled=True)
    feature_grad = (own_share + self_feature).astype(jnp.bfloat16)
    weight_total, self_total = lax.psum((weight_part, self_part), ("row", "col"))
    factor = 1.0 / math.sqrt(node_rows * col_count * row_count)
    return (activations, feature_grad, weight_total * factor, self_total * factor)


def solution(mesh):
    placed = (
        P(("row", "col"), None),
        P(),
        P(),
        P("row", "col", None, None),
        P("row", "col"),
        P("row", "col"),
        P("row", "col"),
        P(("row", "col"), None),
    )
    return jax.shard_map(
        shards,
        mesh=mesh,
        in_specs=placed,
        out_specs=(P(("row", "col"), None), P(("row", "col"), None), P(), P()),
        check_vma=False,
    )
```

profile of v0, /device:TPU:4, one launch (start us, length us, event | category | flops | bytes accessed | tf_op | source)
XLA Modules:
  0.0 519.9 jit_solution(5023080746673470452)
XLA Ops:
  7.2 0.7 all-gather.2.cloned.1.call-update
  8.6 46.0 %all-gather.2.cloned.1.call-done = bf16[2048,256]{1,0:T(8,128)(2,1)} async-done(((bf16[256,256]{1,0:T(8,128)(2,1)}), bf16[2048,256]{1,0:T(8,128)(2,1)}) %all-gather.2.cloned.1.call-update) | async-done | bytes 1048592 | tf_op jit(solution)/shard_map/all_gather | solution.py:43
  54.6 5.8 %collective-permute-start.1 = (bf16[2048,256]{1,0:T(8,128)(2,1)}, bf16[2048,256]{1,0:T(8,128)(2,1)S(1)}, u32[]{:S(2)}, u32[]{:S(2)}) collective-permute-start(bf16[2048,256]{1,0:T(8,128)(2,1)} %all-gather.2.cloned.1.call-done), channel_id=1, source_target_pairs={{8,0},{16,8},{24,16},{32,24},{40,32},{48,40},{56,48},{64,56},{72,6... | collective-permute-start | bytes 3145736 | tf_op jit(solution)/shard_map/ppermute | solution.py:17
  60.5 1.9 collective-permute-start
  62.4 0.7 fusion.16
  63.1 0.7 fusion.17
  63.8 0.7 and_convert_fusion
  64.4 15.8 %collective-permute-done.1 = bf16[2048,256]{1,0:T(8,128)(2,1)S(1)} collective-permute-done((bf16[2048,256]{1,0:T(8,128)(2,1)}, bf16[2048,256]{1,0:T(8,128)(2,1)S(1)}, u32[]{:S(2)}, u32[]{:S(2)}) %collective-permute-start.1) | collective-permute-done | bytes 1048608 | tf_op jit(solution)/shard_map/ppermute | solution.py:17
  80.3 6.1 %collective-permute-done = bf16[2048,256]{1,0:T(8,128)(2,1)S(1)} collective-permute-done((bf16[2048,256]{1,0:T(8,128)(2,1)}, bf16[2048,256]{1,0:T(8,128)(2,1)S(1)}, u32[]{:S(2)}, u32[]{:S(2)}) %collective-permute-start) | collective-permute-done | bytes 1048608 | tf_op jit(solution)/shard_map/ppermute | solution.py:15
  86.4 1.6 pad_maximum_fusion
  88.0 2.0 gather_fusion
  90.1 2.7 fusion.9
  93.0 0.9 multiply_convert_fusion
  94.0 0.2 convolution_convert_fusion
  94.2 0.7 gather_fusion.1
  94.9 0.5 copy-done.1
  95.4 2.9 multiply_bitcast_fusion
  98.3 5.6 %copy.15 = f32[32,128,256]{2,1,0:T(8,128)} copy(f32[32,128,256]{1,2,0:T(8,128)} %multiply_bitcast_fusion) | data formatting | bytes 8388608 | tf_op jit(solution)/shard_map/mul | solution.py:78
  103.9 3.4 broadcast_in_dim.2
  107.3 9.9 %scatter_fusion = f32[48,128,256]{2,1,0:T(8,128)} fusion(f32[48,128,256]{2,1,0:T(8,128)} %broadcast_in_dim.2, s32[32]{0:T(128)S(1)} %fusion.16, f32[32,128,256]{2,1,0:T(8,128)} %copy.15), kind=kCustom, calls=%fused_computation.2 | custom fusion | flops 1048576 | bytes 12583040 | tf_op jit(solution)/shard_map/scatter-add | solution.py:78
  117.3 5.6 %fusion.20 = (f32[16,128,256]{2,1,0:T(8,128)S(1)}, f32[16,128,256]{2,1,0:T(8,128)}, f32[16,128,256]{2,1,0:T(8,128)}) fusion(f32[48,128,256]{2,1,0:T(8,128)} %scatter_fusion), kind=kLoop, calls=%fused_computation.33 | loop fusion | bytes 12582912 | tf_op jit(solution)/shard_map/slice | solution.py:80
  122.9 1.9 collective-permute-start.3
  124.8 3.9 collective-permute-start.2
  128.7 0.9 fusion.23
  129.7 0.9 convolution_bitcast_fusion
  130.7 37.7 %collective-permute-done.3 = f32[2048,256]{1,0:T(8,128)} collective-permute-done((f32[2048,256]{1,0:T(8,128)}, f32[2048,256]{1,0:T(8,128)}, u32[]{:S(2)}, u32[]{:S(2)}) %collective-permute-start.3) | collective-permute-done | bytes 2097184 | tf_op jit(solution)/shard_map/ppermute | solution.py:27
  168.4 4.0 collective-permute-done.2
  172.4 4.0 fusion
  176.6 290.9 %all-reduce.3.cloned.1.call-done = (f32[256,256]{1,0:T(8,128)}, f32[256,256]{1,0:T(8,128)}) async-done(((f32[256,256]{1,0:T(8,128)}, f32[256,256]{1,0:T(8,128)}), (f32[256,256]{1,0:T(8,128)}, f32[256,256]{1,0:T(8,128)})) %all-reduce.3.cloned.1.call-update) | async-done | bytes 524304 | tf_op jit(solution)/shard_map/psum | solution.py:86
  467.5 1.9 broadcast_multiply_fusion
  469.4 42.4 %reduce-scatter.2.cloned.1.call-done = f32[256,256]{1,0:T(8,128)} async-done(((f32[2048,256]{1,0:T(8,128)}), f32[256,256]{1,0:T(8,128)}) %reduce-scatter.2.cloned.1.call-update) | async-done | bytes 262160 | tf_op jit(solution)/shard_map/reduce_scatter | solution.py:84
  511.8 1.6 add_convert_fusion
  (26 shorter events, 0.6 us)
Async XLA Ops:
  7.2 85.8 %copy-start = (bf16[256,256]{1,0:T(8,128)(2,1)S(1)}, bf16[256,256]{1,0:T(8,128)(2,1)}, u32[]{:S(2)}) copy-start(bf16[256,256]{1,0:T(8,128)(2,1)} %param.10) | copy-start | bytes 393220
  7.2 47.5 %all-gather.2.cloned.1.call-start = ((), (), s32[]{:S(2)}) async-start(), calls=%async_computation.1 | async-start | bytes 1179648 | tf_op jit(solution)/shard_map/all_gather | solution.py:43
  7.9 459.6 %all-reduce.3.cloned.1.call-start = ((), (), s32[]{:S(2)}) async-start(), calls=%async_computation.3 | async-start | bytes 1048576 | tf_op jit(solution)/shard_map/psum | solution.py:86
  54.6 25.6 %collective-permute-start.1 = (bf16[2048,256]{1,0:T(8,128)(2,1)}, bf16[2048,256]{1,0:T(8,128)(2,1)S(1)}, u32[]{:S(2)}, u32[]{:S(2)}) collective-permute-start(bf16[2048,256]{1,0:T(8,128)(2,1)} %all-gather.2.cloned.1.call-done), channel_id=1, source_target_pairs={{8,0},{16,8},{24,16},{32,24},{40,32},{48,40},{56,48},{64,56},{72,6... | collective-permute-start | bytes 3145736 | tf_op jit(solution)/shard_map/ppermute | solution.py:17
  60.5 25.9 %collective-permute-start = (bf16[2048,256]{1,0:T(8,128)(2,1)}, bf16[2048,256]{1,0:T(8,128)(2,1)S(1)}, u32[]{:S(2)}, u32[]{:S(2)}) collective-permute-start(bf16[2048,256]{1,0:T(8,128)(2,1)} %all-gather.2.cloned.1.call-done), channel_id=1, source_target_pairs={{0,8},{8,16},{16,24},{24,32},{32,40},{40,48},{48,56},{56,64},{64,7... | collective-permute-start | bytes 3145736 | tf_op jit(solution)/shard_map/ppermute | solution.py:15
  90.1 2.7 copy-start.2
  90.1 2.9 copy-start.3
  90.1 2.9 copy-start.7
  92.8 1.4 copy-start.5
  94.2 1.2 copy-start.1
  117.3 11.4 %copy-start.6 = (bf16[2,128,256]{2,1,0:T(8,128)(2,1)S(1)}, bf16[2,128,256]{2,1,0:T(8,128)(2,1)}, u32[]{:S(2)}) copy-start(bf16[2,128,256]{2,1,0:T(8,128)(2,1)} %copy-done.5) | copy-start | bytes 393220
  117.3 12.4 %copy-start.4 = (bf16[256,256]{1,0:T(8,128)(2,1)S(1)}, bf16[256,256]{1,0:T(8,128)(2,1)}, u32[]{:S(2)}) copy-start(bf16[256,256]{1,0:T(8,128)(2,1)} %param.8) | copy-start | bytes 393220
  122.9 45.5 %collective-permute-start.3 = (f32[2048,256]{1,0:T(8,128)}, f32[2048,256]{1,0:T(8,128)}, u32[]{:S(2)}, u32[]{:S(2)}) collective-permute-start(f32[2048,256]{1,0:T(8,128)} %bitcast.16), channel_id=1, source_target_pairs={{0,504},{8,0},{16,8},{24,16},{32,24},{40,32},{48,40},{56,48},{64,5... | collective-permute-start | bytes 6291464 | tf_op jit(solution)/shard_map/ppermute | solution.py:27
  124.8 47.6 %collective-permute-start.2 = (f32[2048,256]{1,0:T(8,128)}, f32[2048,256]{1,0:T(8,128)}, u32[]{:S(2)}, u32[]{:S(2)}) collective-permute-start(f32[2048,256]{1,0:T(8,128)} %bitcast.15), channel_id=1, source_target_pairs={{0,8},{8,16},{16,24},{24,32},{32,40},{40,48},{48,56},{56,64},{64,7... | collective-permute-start | bytes 6291464 | tf_op jit(solution)/shard_map/ppermute | solution.py:27
  130.6 381.2 %reduce-scatter.2.cloned.1.call-start = ((), (), s32[]{:S(2)}) async-start(), calls=%async_computation.2 | async-start | bytes 2359296 | tf_op jit(solution)/shard_map/reduce_scatter | solution.py:84
Sparse Core Ops, SparseCore 0:
  10.1 44.5 all-gather.1
  130.7 336.7 all-reduce.2
  470.6 41.1 reduce-scatter.1
where the time goes:
time: 520 us
  waiting for transfers between devices  444 us (85%)
  other arithmetic  21 us (4%)
  local copies, waits for them, and re-layouts  17.9 us (3%)
  between operations  14.6 us (3%)
  starting transfers between devices  13.7 us (3%)
  matrix products  9.04 us (2%)
    psum x1, waiting for transfers between devices, shards(): lax.psum((weight_part, self_part), ('row', 'col'))  291 us
    all_gather x1, waiting for transfers between devices, shards(): group = lax.all_gather(features, 'col', axis=0, tiled=True)  46 us
    reduce_scatter x1, waiting for transfers between devices, shards(): own_share = lax.psum_scatter(middle, 'col', scatter_dimension=0, tiled=True)  42.4 us
    ppermute x2, waiting for transfers between devices, passed_along(): return lax.ppermute(value, axis, pairs)  41.7 us
    ppermute x1, waiting for transfers between devices, with_halo(): lax.ppermute(head, axis, [((i + 1) % count, i) for i in range(count)])  15.8 us
  transfers between devices with their start and end apart: 7, of which 7 were waited for; matrix products, arithmetic and copies ran while one was open for 2% of the time, Pallas kernels for 0%

commit v1 on v0

--- a/solution.py
+++ b/solution.py
@@ -83,7 +83,7 @@
         middle = middle + passed_along(outgoing, "row", offset)
     own_share = lax.psum_scatter(middle, "col", scatter_dimension=0, tiled=True)
     feature_grad = (own_share + self_feature).astype(jnp.bfloat16)
-    weight_total, self_total = lax.psum((weight_part, self_part), ("row", "col"))
+    weight_total, self_total = lax.psum(lax.psum((weight_part, self_part), "col"), "row")
     factor = 1.0 / math.sqrt(node_rows * col_count * row_count)
     return (activations, feature_grad, weight_total * factor, self_total * factor)
 

time: 520 us -> 1170 us (2.25)
  the two profiles are of different devices: /device:TPU:4 before, /device:TPU:2 now
where the time goes in v1:
time: 1170 us
  waiting for transfers between devices  1090 us (93%)
  other arithmetic  21.1 us (2%)
  local copies, waits for them, and re-layouts  17.9 us (2%)
  between operations  14.6 us (1%)
  starting transfers between devices  13.8 us (1%)
    psum x1, waiting for transfers between devices, shards(): lax.psum(lax.psum((weight_part, self_part), 'col'), 'row')  816 us
    psum x1, waiting for transfers between devices, shards(): lax.psum((weight_part, self_part), 'col')  145 us
    reduce_scatter x1, waiting for transfers between devices, shards(): own_share = lax.psum_scatter(middle, 'col', scatter_dimension=0, tiled=True)  63.2 us
    all_gather x1, waiting for transfers between devices, shards(): group = lax.all_gather(features, 'col', axis=0, tiled=True)  46.1 us
  transfers between devices with their start and end apart: 8, of which 6 were waited for; matrix products, arithmetic and copies ran while one was open for 1% of the time, Pallas kernels for 0%

profile of v1, /device:TPU:2, one launch (start us, length us, event | category | flops | bytes accessed | tf_op | source)
XLA Modules:
  0.0 1168.9 jit_solution(9385190563962858838)
XLA Ops:
  7.2 0.7 all-gather.2.cloned.1.call-update
  8.6 46.1 %all-gather.2.cloned.1.call-done = bf16[2048,256]{1,0:T(8,128)(2,1)} async-done(((bf16[256,256]{1,0:T(8,128)(2,1)}), bf16[2048,256]{1,0:T(8,128)(2,1)}) %all-gather.2.cloned.1.call-update) | async-done | bytes 1048592 | tf_op jit(solution)/shard_map/all_gather | solution.py:43
  54.7 5.8 collective-permute-start.1
  60.5 1.9 collective-permute-start
  62.5 0.7 fusion.16
  63.1 0.7 fusion.17
  63.8 0.7 and_convert_fusion
  64.5 15.8 %collective-permute-done.1 = bf16[2048,256]{1,0:T(8,128)(2,1)S(1)} collective-permute-done((bf16[2048,256]{1,0:T(8,128)(2,1)}, bf16[2048,256]{1,0:T(8,128)(2,1)S(1)}, u32[]{:S(2)}, u32[]{:S(2)}) %collective-permute-start.1) | collective-permute-done | bytes 1048608 | tf_op jit(solution)/shard_map/ppermute | solution.py:17
  80.3 6.1 collective-permute-done
  86.4 1.6 pad_maximum_fusion
  88.0 2.0 gather_fusion
  90.1 2.7 fusion.9
  93.0 0.9 multiply_convert_fusion
  94.0 0.2 convolution_convert_fusion
  94.2 0.7 gather_fusion.1
  94.9 0.5 copy-done.1
  95.4 2.9 multiply_bitcast_fusion
  98.3 5.6 copy.15
  103.9 3.4 broadcast_in_dim.2
  107.4 10.1 scatter_fusion
  117.4 5.6 fusion.20
  123.0 1.9 collective-permute-start.3
  124.9 3.9 collective-permute-start.2
  128.9 0.9 fusion.23
  129.8 0.9 convolution_bitcast_fusion
  130.8 144.8 %all-reduce.7.cloned.1.call-done = (f32[256,256]{1,0:T(8,128)}, f32[256,256]{1,0:T(8,128)}) async-done(((f32[256,256]{1,0:T(8,128)}, f32[256,256]{1,0:T(8,128)}), (f32[256,256]{1,0:T(8,128)}, f32[256,256]{1,0:T(8,128)})) %all-reduce.7.cloned.1.call-update) | async-done | bytes 524304 | tf_op jit(solution)/shard_map/psum | solution.py:86
  275.7 4.0 fusion
  279.7 0.2 fusion.22
  279.9 815.8 %all-reduce.5.cloned.1.call-done = (f32[256,256]{1,0:T(8,128)}, f32[256,256]{1,0:T(8,128)}) async-done(((f32[256,256]{1,0:T(8,128)}, f32[256,256]{1,0:T(8,128)}), (f32[256,256]{1,0:T(8,128)}, f32[256,256]{1,0:T(8,128)})) %all-reduce.5.cloned.1.call-update) | async-done | bytes 524304 | tf_op jit(solution)/shard_map/psum | solution.py:86
  1095.7 1.9 broadcast_multiply_fusion
  1097.6 63.2 %reduce-scatter.2.cloned.1.call-done = f32[256,256]{1,0:T(8,128)} async-done(((f32[2048,256]{1,0:T(8,128)}), f32[256,256]{1,0:T(8,128)}) %reduce-scatter.2.cloned.1.call-update) | async-done | bytes 262160 | tf_op jit(solution)/shard_map/reduce_scatter | solution.py:84
  1160.7 1.6 add_convert_fusion
  (29 shorter events, 0.5 us)
Async XLA Ops:
  7.2 85.8 %copy-start = (bf16[256,256]{1,0:T(8,128)(2,1)S(1)}, bf16[256,256]{1,0:T(8,128)(2,1)}, u32[]{:S(2)}) copy-start(bf16[256,256]{1,0:T(8,128)(2,1)} %param.10) | copy-start | bytes 393220
  7.2 47.5 %all-gather.2.cloned.1.call-start = ((), (), s32[]{:S(2)}) async-start(), calls=%async_computation.1 | async-start | bytes 1179648 | tf_op jit(solution)/shard_map/all_gather | solution.py:43
  7.9 267.7 %all-reduce.7.cloned.1.call-start = ((), (), s32[]{:S(2)}) async-start(), calls=%async_computation.4 | async-start | bytes 1048576 | tf_op jit(solution)/shard_map/psum | solution.py:86
  54.7 25.6 %collective-permute-start.1 = (bf16[2048,256]{1,0:T(8,128)(2,1)}, bf16[2048,256]{1,0:T(8,128)(2,1)S(1)}, u32[]{:S(2)}, u32[]{:S(2)}) collective-permute-start(bf16[2048,256]{1,0:T(8,128)(2,1)} %all-gather.2.cloned.1.call-done), channel_id=1, source_target_pairs={{8,0},{16,8},{24,16},{32,24},{40,32},{48,40},{56,48},{64,56},{72,6... | collective-permute-start | bytes 3145736 | tf_op jit(solution)/shard_map/ppermute | solution.py:17
  60.5 25.9 %collective-permute-start = (bf16[2048,256]{1,0:T(8,128)(2,1)}, bf16[2048,256]{1,0:T(8,128)(2,1)S(1)}, u32[]{:S(2)}, u32[]{:S(2)}) collective-permute-start(bf16[2048,256]{1,0:T(8,128)(2,1)} %all-gather.2.cloned.1.call-done), channel_id=1, source_target_pairs={{0,8},{8,16},{16,24},{24,32},{32,40},{40,48},{48,56},{56,64},{64,7... | collective-permute-start | bytes 3145736 | tf_op jit(solution)/shard_map/ppermute | solution.py:15
  90.1 2.7 copy-start.2
  90.1 2.9 copy-start.3
  90.1 2.9 copy-start.7
  92.8 1.4 copy-start.5
  94.2 1.2 copy-start.1
  117.4 11.4 copy-start.6
  117.4 12.4 %copy-start.4 = (bf16[256,256]{1,0:T(8,128)(2,1)S(1)}, bf16[256,256]{1,0:T(8,128)(2,1)}, u32[]{:S(2)}) copy-start(bf16[256,256]{1,0:T(8,128)(2,1)} %param.8) | copy-start | bytes 393220
  123.0 152.6 %collective-permute-start.3 = (f32[2048,256]{1,0:T(8,128)}, f32[2048,256]{1,0:T(8,128)}, u32[]{:S(2)}, u32[]{:S(2)}) collective-permute-start(f32[2048,256]{1,0:T(8,128)} %bitcast.16), channel_id=1, source_target_pairs={{0,504},{8,0},{16,8},{24,16},{32,24},{40,32},{48,40},{56,48},{64,5... | collective-permute-start | bytes 6291464 | tf_op jit(solution)/shard_map/ppermute | solution.py:27
  124.9 150.7 %collective-permute-start.2 = (f32[2048,256]{1,0:T(8,128)}, f32[2048,256]{1,0:T(8,128)}, u32[]{:S(2)}, u32[]{:S(2)}) collective-permute-start(f32[2048,256]{1,0:T(8,128)} %bitcast.15), channel_id=1, source_target_pairs={{0,8},{8,16},{16,24},{24,32},{32,40},{40,48},{48,56},{56,64},{64,7... | collective-permute-start | bytes 6291464 | tf_op jit(solution)/shard_map/ppermute | solution.py:27
  130.8 964.9 %all-reduce.5.cloned.1.call-start = ((), (), s32[]{:S(2)}) async-start(), calls=%async_computation.3 | async-start | bytes 1048576 | tf_op jit(solution)/shard_map/psum | solution.py:86
  275.6 885.1 %reduce-scatter.2.cloned.1.call-start = ((), (), s32[]{:S(2)}) async-start(), calls=%async_computation.2 | async-start | bytes 2359296 | tf_op jit(solution)/shard_map/reduce_scatter | solution.py:84
Sparse Core Ops, SparseCore 0:
  10.1 44.5 all-gather.1
  130.9 144.6 all-reduce.6
  278.8 816.8 all-reduce.4
  1098.4 62.2 reduce-scatter.1
